TPU v7x, 32 devices: a whole 2x2x4 slice. The times are simulated.
32 devices in a mesh: dp: 4 (over y, core), slab: 8 (over z, x).
Axes of the slice: x: 2, y: 2, z: 4, core: 2. Of those that a mesh axis runs over, the one named last changes fastest.
Arguments:
- features: bfloat16 [4, 64, 256, 8, 256], P('dp', None, 'slab'), may hold values from -6 to 6
- target: bfloat16 [4, 256, 8, 256], P('dp', 'slab'), may hold values from -6 to 6
- out_weight: float32 [64], replicated, may hold values from -1.5 to 1.5
- rotation: int32 [4], P('dp'), may hold values from 0 to 3
- blocks: int32 [8, 2], replicated, may hold values from 0 to 3, as said below
- wedge: int32 [256, 256], replicated, may hold values 0 or 1
Outputs:
- vol_grad: float32 [4, 256, 8, 256], P('dp', 'slab')
- w_grad: float32 [64], replicated
Inputs may be any that keep to these rules, and one draw needn't show every extreme that they name: `blocks`: the 8 rows are distinct pairs of block indices of the frequency plane, each from 0 to 3.
All inputs are finite; a program needn't handle non-finite values.
Results may differ from a plain program's by a relative error of at most 0.0003.
Values sent between devices are 32-bit elements; how exact they have to be, the bound alone decides.
A program may use at most 64 MiB of HBM per device.

v0:
```python
import functools
import math

import numpy as np

import jax
import jax.numpy as jnp
from jax import lax
from jax.experimental import pallas as pl
from jax.experimental.pallas import tpu as pltpu
from jax.sharding import PartitionSpec as P

BLK = 64
ROWS = 8
MESH = pl.DeviceIdType.MESH


def product(form, left, right):
    return jnp.einsum(form, left, right, precision=lax.Precision.HIGHEST)


def wedge_weights(blocks, wedge, length):
    per_side = length // BLK
    labels = jnp.arange(per_side, dtype=jnp.int32)
    match = (blocks[:, 0][:, None, None] == labels[None, :, None]) & (
        blocks[:, 1][:, None, None] == labels[None, None, :]
    )
    listed = jnp.any(match, axis=0)
    spread = jnp.repeat(jnp.repeat(listed, BLK, axis=0), BLK, axis=1)
    return jnp.where(spread, wedge, 0).astype(jnp.float32)


def phase_tables(turns, length):
    positions = jnp.arange(length, dtype=jnp.int32)
    flip_depth = turns >= 2
    flip_width = (turns == 1) | (turns == 2)
    depth_index = jnp.where(
        flip_depth[:, None], length - 1 - positions[None, :], positions[None, :]
    )
    width_index = jnp.where(
        flip_width[:, None], length - 1 - positions[None, :], positions[None, :]
    )
    depth_phase = positions[None, :, None] * depth_index[:, None, :] % length
    width_phase = width_index[:, :, None] * positions[None, None, :] % length
    depth_angle = depth_phase.astype(jnp.float32) * (2.0 * math.pi / length)
    width_angle = width_phase.astype(jnp.float32) * (2.0 * math.pi / length)
    return (jnp.cos(depth_angle), jnp.sin(depth_angle), jnp.cos(width_angle), jnp.sin(width_angle))


def split_lines(features, target, out_weight, rotation, blocks, wedge):
    length = features.shape[-1]
    plane_count = features.shape[3]
    slab_count = lax.axis_size("slab")
    columns = length // slab_count
    col_start = lax.axis_index("slab") * columns
    features_wide = features.astype(jnp.float32)
    volume = product("c,sczyx->szyx", out_weight, features_wide)
    difference = volume - target.astype(jnp.float32)
    depth_cos, depth_sin, width_cos, width_sin = phase_tables(rotation, length)
    line_real = product("szyb,sbp->szyp", difference, width_cos)
    line_imag = -product("szyb,sbp->szyp", difference, width_sin)
    line_real, line_imag = (
        lax.all_to_all(line_real, "slab", split_axis=3, concat_axis=1, tiled=True),
        lax.all_to_all(line_imag, "slab", split_axis=3, concat_axis=1, tiled=True),
    )
    spec_real = (
        product("spa,sayq->spyq", depth_cos, line_real)
        + product("spa,sayq->spyq", depth_sin, line_imag)
    ) / length
    spec_imag = (
        product("spa,sayq->spyq", depth_cos, line_imag)
        - product("spa,sayq->spyq", depth_sin, line_real)
    ) / length
    mask = wedge_weights(blocks, wedge, length)
    odd_turn = rotation % 2 == 1
    mask_turned = jnp.where(odd_turn[:, None, None], mask.T[None], mask[None])
    mask_columns = lax.dynamic_slice_in_dim(mask_turned, col_start, columns, 2)
    grad_real = 2.0 * mask_columns[:, :, None, :] * spec_real
    grad_imag = 2.0 * mask_columns[:, :, None, :] * spec_imag
    back_real = product("spa,spyq->sayq", depth_cos, grad_real) - product(
        "spa,spyq->sayq", depth_sin, grad_imag
    )
    back_imag = product("spa,spyq->sayq", depth_cos, grad_imag) + product(
        "spa,spyq->sayq", depth_sin, grad_real
    )
    back_real, back_imag = (
        lax.all_to_all(back_real, "slab", split_axis=1, concat_axis=3, tiled=True),
        lax.all_to_all(back_imag, "slab", split_axis=1, concat_axis=3, tiled=True),
    )
    vol_grad = (
        product("sayp,sbp->sayb", back_real, width_cos)
        - product("sayp,sbp->sayb", back_imag, width_sin)
    ) / length
    voxel_count = lax.axis_size("dp") * features.shape[0] * length * plane_count * length
    local_sum = product("sczyx,szyx->c", features_wide, vol_grad) / voxel_count
    w_grad = lax.psum(local_sum, ("dp", "slab"))
    return (vol_grad, w_grad)


def hartley_tables(length):
    index = np.arange(length)
    angle = (index[:, None] * index[None, :] % length) * (2.0 * np.pi / length)
    cos, sin = np.cos(angle), np.sin(angle)
    parts = []
    for table in (cos, sin, cos + sin, cos - sin):
        high = table.astype(jnp.bfloat16)
        parts += [high, (table - high.astype(np.float64)).astype(jnp.bfloat16)]
    return np.stack(parts)


def halves(value):
    high = value.astype(jnp.bfloat16)
    return high, (value - high.astype(jnp.float32)).astype(jnp.bfloat16)


def dot(left, right):
    return jnp.dot(left, right, preferred_element_type=jnp.float32)


def dot3(left, right):
    return dot(left[0], right[0]) + (dot(left[0], right[1]) + dot(left[1], right[0]))


def kernel(
    dp_count, slab_count, voxel_count,
    weight, rotation, blocks, features_hbm, target_hbm, wedge_hbm, tables_hbm,
    out, out_weight_grad,
    features, target, wedge, tables, outgoing, plane, filt, back, returned, sums, own_sum, all_sums,
    load_sem, side_sem, send_sem, recv_sem, send2_sem, recv2_sem, sum_send_sem, sum_recv_sem,
):
    channels, depth, planes, length = features.shape
    pieces = depth // ROWS
    my_dp, me = lax.axis_index("dp"), lax.axis_index("slab")
    total = dp_count * slab_count

    def other(offset):
        place = lax.rem(my_dp * slab_count + me + offset, total)
        return (lax.div(place, slab_count), lax.rem(place, slab_count))

    loads = []
    for j in range(pieces):
        rows = pl.ds(j * ROWS, ROWS)
        loads.append(pltpu.make_async_copy(features_hbm.at[:, rows], features.at[:, rows], load_sem.at[j]))
    sides = [
        pltpu.make_async_copy(target_hbm, target, side_sem.at[0]),
        pltpu.make_async_copy(wedge_hbm, wedge, side_sem.at[1]),
        pltpu.make_async_copy(tables_hbm, tables, side_sem.at[2]),
    ]
    sides[0].start()
    for copy in loads:
        copy.start()
    for copy in sides[1:]:
        copy.start()

    barrier = pltpu.get_barrier_semaphore()
    for offset in range(1, total):
        pl.semaphore_signal(barrier, inc=1, device_id=other(offset), device_id_type=MESH)

    sends = []
    for j in range(pieces):
        loads[j].wait()
        if j == 0:
            sides[0].wait()
        base = j * ROWS

        def add_channel(c, accs):
            scale = weight[c]
            return tuple(
                accs[z] + scale * features[c, base + z].astype(jnp.float32) for z in range(ROWS)
            )

        start = tuple(-target[base + z].astype(jnp.float32) for z in range(ROWS))
        accs = lax.fori_loop(0, channels, add_channel, start, unroll=4)
        piece = jnp.swapaxes(jnp.stack(accs, axis=0), 0, 1)
        outgoing[:, pl.ds(base, ROWS), :] = piece
        if j == 0:
            pl.semaphore_wait(barrier, total - 1)
        for r in range(1, slab_count):
            peer = lax.rem(me + r, slab_count)
            copy = pltpu.make_async_remote_copy(
                src_ref=outgoing.at[peer, pl.ds(base, ROWS)],
                dst_ref=plane.at[pl.ds(pl.multiple_of(me * depth + base, ROWS), ROWS)],
                send_sem=send_sem.at[r - 1, j],
                recv_sem=recv_sem.at[r - 1, j],
                device_id=(my_dp, peer),
                device_id_type=MESH,
            )
            copy.start()
            sends.append(copy)
        plane[pl.ds(pl.multiple_of(me * depth + base, ROWS), ROWS), :] = outgoing[me, pl.ds(base, ROWS), :]

    sides[1].wait()
    row = lax.broadcasted_iota(jnp.int32, (length, length), 0)
    column = lax.broadcasted_iota(jnp.int32, (length, length), 1)
    row_block, column_block = row // BLK, column // BLK
    listed = jnp.zeros((length, length), jnp.bool_)
    for n in range(blocks.shape[1]):
        listed = listed | ((row_block == blocks[0, n]) & (column_block == blocks[1, n]))
    mask = jnp.where(listed, wedge[...], 0).astype(jnp.float32)
    mirror = jnp.where(lax.rem(row + column, length) == 0, 1.0, 0.0).astype(jnp.bfloat16)
    flipped = dot(dot(mirror, mask.astype(jnp.bfloat16)).astype(jnp.bfloat16), mirror)
    even = mask + flipped
    odd = lax.dot_general(
        even.astype(jnp.bfloat16), mirror, (((0,), (0,)), ((), ())), preferred_element_type=jnp.float32
    )
    is_odd = lax.rem(rotation[0], 2) == 1
    filt[...] = jnp.where(is_odd, odd, even) * (1.0 / (length * length))
    sides[2].wait()

    for copy in sends:
        copy.wait()

    def table(k):
        return tables[2 * k], tables[2 * k + 1]

    values = halves(plane[...])
    first, second = halves(dot3(values, table(2))), halves(dot3(values, table(3)))
    spectrum = dot3(table(0), first) + dot3(table(1), second)
    kept = halves(spectrum * filt[...])
    first, second = halves(dot3(table(0), kept)), halves(dot3(table(1), kept))
    back[...] = dot3(first, table(2)) + dot3(second, table(3))

    sends = []
    for r in range(1, slab_count):
        peer = lax.rem(me + r, slab_count)
        copy = pltpu.make_async_remote_copy(
            src_ref=back.at[pl.ds(pl.multiple_of(peer * depth, ROWS), depth)],
            dst_ref=returned.at[me],
            send_sem=send2_sem.at[r - 1],
            recv_sem=recv2_sem.at[r - 1],
            device_id=(my_dp, peer),
            device_id_type=MESH,
        )
        copy.start()
        sends.append(copy)
    returned[me] = back[pl.ds(pl.multiple_of(me * depth, ROWS), depth), :]
    for copy in sends:
        copy.wait()

    for j in range(pieces):
        base = j * ROWS
        piece = jnp.swapaxes(returned[:, pl.ds(base, ROWS), :], 0, 1)
        out[pl.ds(base, ROWS)] = piece
        grads = [piece[z] for z in range(ROWS)]

        def channel_sum(c, carry):
            acc = grads[0] * features[c, base].astype(jnp.float32)
            for z in range(1, ROWS):
                acc = acc + grads[z] * features[c, base + z].astype(jnp.float32)
            folded = acc[:, :128]
            for lane in range(128, length, 128):
                folded = folded + acc[:, lane:lane + 128]
            sums[c] = folded if j == 0 else sums[c] + folded
            return carry

        lax.fori_loop(0, channels, channel_sum, 0, unroll=4)

    rest = jnp.sum(sums[...], axis=1)
    ones = jnp.ones((8, 128), jnp.bfloat16)
    row_sum = jnp.zeros((8, channels), jnp.float32)
    for _ in range(3):
        part = rest.astype(jnp.bfloat16)
        rest = rest - part.astype(jnp.float32)
        row_sum = row_sum + lax.dot_general(
            ones, part, (((1,), (1,)), ((), ())), preferred_element_type=jnp.float32
        )
    row_sum = row_sum[0:1]
    own_sum[0] = row_sum
    place = my_dp * slab_count + me
    sends = []
    for offset in range(1, total):
        copy = pltpu.make_async_remote_copy(
            src_ref=own_sum.at[0],
            dst_ref=all_sums.at[place],
            send_sem=sum_send_sem.at[offset - 1],
            recv_sem=sum_recv_sem.at[offset - 1],
            device_id=other(offset),
            device_id_type=MESH,
        )
        copy.start()
        sends.append(copy)
    all_sums[place] = row_sum
    for copy in sends:
        copy.wait()
    out_weight_grad[...] = jnp.sum(all_sums[...], axis=0) / voxel_count


def split_planes(features, target, out_weight, rotation, blocks, wedge):
    _, channels, depth, planes, length = features.shape
    dp_count, slab_count = lax.axis_size("dp"), lax.axis_size("slab")
    total = dp_count * slab_count
    pieces = depth // ROWS
    voxel_count = dp_count * length * planes * length
    smem = pl.BlockSpec(memory_space=pltpu.SMEM)
    hbm = pl.BlockSpec(memory_space=pltpu.HBM)
    vmem = pl.BlockSpec(memory_space=pltpu.VMEM)
    dma = pltpu.SemaphoreType.DMA
    vol_grad, w_grad = pl.pallas_call(
        functools.partial(kernel, dp_count, slab_count, float(voxel_count)),
        out_shape=(
            jax.ShapeDtypeStruct((depth, planes, length), jnp.float32),
            jax.ShapeDtypeStruct((1, channels), jnp.float32),
        ),
        in_specs=[smem, smem, smem, hbm, hbm, hbm, hbm],
        out_specs=(vmem, vmem),
        scratch_shapes=[
            pltpu.VMEM((channels, depth, planes, length), jnp.bfloat16),
            pltpu.VMEM((depth, planes, length), jnp.bfloat16),
            pltpu.VMEM((length, length), jnp.int32),
            pltpu.VMEM((8, length, length), jnp.bfloat16),
            pltpu.VMEM((planes, depth, length), jnp.float32),
            pltpu.VMEM((length, length), jnp.float32),
            pltpu.VMEM((length, length), jnp.float32),
            pltpu.VMEM((length, length), jnp.float32),
            pltpu.VMEM((planes, depth, length), jnp.float32),
            pltpu.VMEM((channels, 8, 128), jnp.float32),
            pltpu.VMEM((1, 1, channels), jnp.float32),
            pltpu.VMEM((total, 1, channels), jnp.float32),
            dma((pieces,)),
            dma((3,)),
            dma((slab_count - 1, pieces)),
            dma((slab_count - 1, pieces)),
            dma((slab_count - 1,)),
            dma((slab_count - 1,)),
            dma((total - 1,)),
            dma((total - 1,)),
        ],
        compiler_params=pltpu.CompilerParams(
            collective_id=0, has_side_effects=True, vmem_limit_bytes=56 * 1024 * 1024
        ),
    )(
        out_weight, rotation, blocks.T, features[0], target[0], wedge, jnp.asarray(hartley_tables(length)),
    )
    return vol_grad[None], w_grad[0]


def solution(mesh):
    def on_device(features, *rest):
        samples, _, depth, planes, length = features.shape
        whole_planes = (
            samples == 1
            and planes == 8
            and planes == mesh.shape["slab"]
            and depth % ROWS == 0
            and length % 128 == 0
        )
        return (split_planes if whole_planes else split_lines)(features, *rest)

    in_specs = (
        P("dp", None, "slab", None, None),
        P("dp", "slab", None, None),
        P(),
        P("dp"),
        P(),
        P(),
    )
    out_specs = (P("dp", "slab", None, None), P())
    return jax.shard_map(
        on_device, mesh=mesh, in_specs=in_specs, out_specs=out_specs, check_vma=False
    )
```

profile of v0, /device:TPU:0, one launch (start us, length us, event | category | flops | bytes accessed | tf_op | source)
XLA Modules:
  0.0 36.8 jit_solution(10776417730460301406)
XLA Ops:
  1.3 32.7 %shard_map.86 = (f32[32,8,256]{2,1,0:T(8,128)}, f32[1,64]{1,0:T(1,128)}) custom-call(f32[64]{0:T(128)} %weight.1, s32[1]{0:T(128)S(6)} %copy.11.rotation, s32[2,8]{1,0:T(2,128)} %bitcast.8, bf16[64,32,8,256]{3,2,1,0:T(8,128)(2,1)} %bitcast.5, bf16[32,8,256]{2,1,0:T(8,128)(2,1)} %bitcast.7, s32[256,256]{1,0:T(8,128)} %wedge_hbm.1, ...), custom_call_target="tpu_custom_call" | custom-call | tf_op jit(solution)/shard_map/pallas_call | solution.py:298
  34.0 1.7 %copy.12 = f32[1,32,8,256]{3,2,1,0:T(8,128)} copy(f32[1,32,8,256]{3,2,1,0:T(8,128)} %bitcast.6) | data formatting | bytes 524288
  35.7 1.1 %copy.13 = f32[64]{0:T(128)} copy(f32[64]{0:T(128)} %bitcast.9) | data formatting | bytes 512
where the time goes:
time: 37 us; the launch traced here: 36.8 us
  Pallas kernels  32.7 us (88%)
  local copies, waits for them, and re-layouts  2.8 us (8%)
  between operations  1.29 us (3%)
    pallas_call x1, Pallas kernels, split_planes(): pl.pallas_call(functools.partial(kernel, dp_count, slab_count, float(voxe...  32.7 us
    unnamed x2, local copies, waits for them, and re-layouts  2.8 us

commit v1 on v0

--- a/solution.py
+++ b/solution.py
@@ -12,6 +12,7 @@
 
 BLK = 64
 ROWS = 8
+HELD = 2
 MESH = pl.DeviceIdType.MESH
 
 
@@ -124,18 +125,20 @@
 def kernel(
     dp_count, slab_count, voxel_count,
     weight, rotation, blocks, features_hbm, target_hbm, wedge_hbm, tables_hbm,
-    out, out_weight_grad,
-    features, target, wedge, tables, outgoing, plane, filt, back, returned, sums, own_sum, all_sums,
-    load_sem, side_sem, send_sem, recv_sem, send2_sem, recv2_sem, sum_send_sem, sum_recv_sem,
+    out_hbm, out_sums,
+    features, target, wedge, tables, out, outgoing, plane, filt, back, returned, sums, own_sum, slab_sums, dp_sums,
+    load_sem, side_sem, send_sem, recv_sem, send2_sem, recv2_sem, sum_send_sem, sum_recv_sem, dp_send_sem, dp_recv_sem,
 ):
     channels, depth, planes, length = features.shape
     pieces = depth // ROWS
     my_dp, me = lax.axis_index("dp"), lax.axis_index("slab")
-    total = dp_count * slab_count
-
-    def other(offset):
-        place = lax.rem(my_dp * slab_count + me + offset, total)
-        return (lax.div(place, slab_count), lax.rem(place, slab_count))
+    slab_steps = range(slab_count - 1, 0, -1)
+
+    def slab_peer(step):
+        return lax.bitwise_xor(me, jnp.int32(step))
+
+    def dp_peer(step):
+        return lax.rem(my_dp + step, dp_count)
 
     loads = []
     for j in range(pieces):
@@ -153,8 +156,10 @@
         copy.start()
 
     barrier = pltpu.get_barrier_semaphore()
-    for offset in range(1, total):
-        pl.semaphore_signal(barrier, inc=1, device_id=other(offset), device_id_type=MESH)
+    for r in slab_steps:
+        pl.semaphore_signal(barrier, inc=1, device_id=(my_dp, slab_peer(r)), device_id_type=MESH)
+    for r in range(1, dp_count):
+        pl.semaphore_signal(barrier, inc=1, device_id=(dp_peer(r), me), device_id_type=MESH)
 
     sends = []
     for j in range(pieces):
@@ -173,13 +178,19 @@
         accs = lax.fori_loop(0, channels, add_channel, start, unroll=4)
         piece = jnp.swapaxes(jnp.stack(accs, axis=0), 0, 1)
         outgoing[:, pl.ds(base, ROWS), :] = piece
-        if j == 0:
-            pl.semaphore_wait(barrier, total - 1)
-        for r in range(1, slab_count):
-            peer = lax.rem(me + r, slab_count)
+        plane[pl.ds(pl.multiple_of(me * depth + base, ROWS), ROWS), :] = outgoing[me, pl.ds(base, ROWS), :]
+        if j < min(HELD, pieces) - 1:
+            continue
+        first = j
+        if j == min(HELD, pieces) - 1:
+            pl.semaphore_wait(barrier, slab_count + dp_count - 2)
+            first = 0
+        rows = pl.ds(first * ROWS, (j + 1 - first) * ROWS)
+        for r in slab_steps:
+            peer = slab_peer(r)
             copy = pltpu.make_async_remote_copy(
-                src_ref=outgoing.at[peer, pl.ds(base, ROWS)],
-                dst_ref=plane.at[pl.ds(pl.multiple_of(me * depth + base, ROWS), ROWS)],
+                src_ref=outgoing.at[peer, rows],
+                dst_ref=plane.at[pl.ds(pl.multiple_of(me * depth + first * ROWS, ROWS), (j + 1 - first) * ROWS)],
                 send_sem=send_sem.at[r - 1, j],
                 recv_sem=recv_sem.at[r - 1, j],
                 device_id=(my_dp, peer),
@@ -187,7 +198,6 @@
             )
             copy.start()
             sends.append(copy)
-        plane[pl.ds(pl.multiple_of(me * depth + base, ROWS), ROWS), :] = outgoing[me, pl.ds(base, ROWS), :]
 
     sides[1].wait()
     row = lax.broadcasted_iota(jnp.int32, (length, length), 0)
@@ -221,24 +231,26 @@
     back[...] = dot3(first, table(2)) + dot3(second, table(3))
 
     sends = []
-    for r in range(1, slab_count):
-        peer = lax.rem(me + r, slab_count)
-        copy = pltpu.make_async_remote_copy(
-            src_ref=back.at[pl.ds(pl.multiple_of(peer * depth, ROWS), depth)],
-            dst_ref=returned.at[me],
-            send_sem=send2_sem.at[r - 1],
-            recv_sem=recv2_sem.at[r - 1],
-            device_id=(my_dp, peer),
-            device_id_type=MESH,
-        )
-        copy.start()
-        sends.append(copy)
+    for j in range(pieces):
+        sends.append([])
+        for r in slab_steps:
+            peer = slab_peer(r)
+            copy = pltpu.make_async_remote_copy(
+                src_ref=back.at[pl.ds(pl.multiple_of(peer * depth + j * ROWS, ROWS), ROWS)],
+                dst_ref=returned.at[me, pl.ds(j * ROWS, ROWS)],
+                send_sem=send2_sem.at[r - 1, j],
+                recv_sem=recv2_sem.at[r - 1, j],
+                device_id=(my_dp, peer),
+                device_id_type=MESH,
+            )
+            copy.start()
+            sends[j].append(copy)
     returned[me] = back[pl.ds(pl.multiple_of(me * depth, ROWS), depth), :]
-    for copy in sends:
-        copy.wait()
 
     for j in range(pieces):
         base = j * ROWS
+        for copy in sends[j]:
+            copy.wait()
         piece = jnp.swapaxes(returned[:, pl.ds(base, ROWS), :], 0, 1)
         out[pl.ds(base, ROWS)] = piece
         grads = [piece[z] for z in range(ROWS)]
@@ -254,6 +266,8 @@
             return carry
 
         lax.fori_loop(0, channels, channel_sum, 0, unroll=4)
+    stored = pltpu.make_async_copy(out, out_hbm, side_sem.at[3])
+    stored.start()
 
     rest = jnp.sum(sums[...], axis=1)
     ones = jnp.ones((8, 128), jnp.bfloat16)
@@ -266,29 +280,50 @@
         )
     row_sum = row_sum[0:1]
     own_sum[0] = row_sum
-    place = my_dp * slab_count + me
     sends = []
-    for offset in range(1, total):
+    for r in slab_steps:
         copy = pltpu.make_async_remote_copy(
             src_ref=own_sum.at[0],
-            dst_ref=all_sums.at[place],
-            send_sem=sum_send_sem.at[offset - 1],
-            recv_sem=sum_recv_sem.at[offset - 1],
-            device_id=other(offset),
+            dst_ref=slab_sums.at[me],
+            send_sem=sum_send_sem.at[r - 1],
+            recv_sem=sum_recv_sem.at[r - 1],
+            device_id=(my_dp, slab_peer(r)),
             device_id_type=MESH,
         )
         copy.start()
         sends.append(copy)
-    all_sums[place] = row_sum
+    slab_sums[me] = row_sum
     for copy in sends:
         copy.wait()
-    out_weight_grad[...] = jnp.sum(all_sums[...], axis=0) / voxel_count
+    row_sum = jnp.sum(slab_sums[...], axis=0)
+    own_sum[1] = row_sum
+    sends = []
+    for r in range(1, dp_count):
+        copy = pltpu.make_async_remote_copy(
+            src_ref=own_sum.at[1],
+            dst_ref=dp_sums.at[my_dp],
+            send_sem=dp_send_sem.at[r - 1],
+            recv_sem=dp_recv_sem.at[r - 1],
+            device_id=(dp_peer(r), me),
+            device_id_type=MESH,
+        )
+        copy.start()
+        sends.append(copy)
+    dp_sums[my_dp] = row_sum
+    for copy in sends:
+        copy.wait()
+    out_sums[...] = jnp.sum(dp_sums[...], axis=0) / voxel_count
+    stored.wait()
+
+
+def hand_over(vol_grad, w_grad, out, out_weight_grad):
+    out[...] = vol_grad[...]
+    out_weight_grad[...] = w_grad[...]
 
 
 def split_planes(features, target, out_weight, rotation, blocks, wedge):
     _, channels, depth, planes, length = features.shape
     dp_count, slab_count = lax.axis_size("dp"), lax.axis_size("slab")
-    total = dp_count * slab_count
     pieces = depth // ROWS
     voxel_count = dp_count * length * planes * length
     smem = pl.BlockSpec(memory_space=pltpu.SMEM)
@@ -302,28 +337,32 @@
             jax.ShapeDtypeStruct((1, channels), jnp.float32),
         ),
         in_specs=[smem, smem, smem, hbm, hbm, hbm, hbm],
-        out_specs=(vmem, vmem),
+        out_specs=(hbm, vmem),
         scratch_shapes=[
             pltpu.VMEM((channels, depth, planes, length), jnp.bfloat16),
             pltpu.VMEM((depth, planes, length), jnp.bfloat16),
             pltpu.VMEM((length, length), jnp.int32),
             pltpu.VMEM((8, length, length), jnp.bfloat16),
+            pltpu.VMEM((depth, planes, length), jnp.float32),
             pltpu.VMEM((planes, depth, length), jnp.float32),
             pltpu.VMEM((length, length), jnp.float32),
             pltpu.VMEM((length, length), jnp.float32),
             pltpu.VMEM((length, length), jnp.float32),
             pltpu.VMEM((planes, depth, length), jnp.float32),
             pltpu.VMEM((channels, 8, 128), jnp.float32),
-            pltpu.VMEM((1, 1, channels), jnp.float32),
-            pltpu.VMEM((total, 1, channels), jnp.float32),
+            pltpu.VMEM((2, 1, channels), jnp.float32),
+            pltpu.VMEM((slab_count, 1, channels), jnp.float32),
+            pltpu.VMEM((dp_count, 1, channels), jnp.float32),
             dma((pieces,)),
-            dma((3,)),
+            dma((4,)),
+            dma((slab_count - 1, pieces)),
+            dma((slab_count - 1, pieces)),
             dma((slab_count - 1, pieces)),
             dma((slab_count - 1, pieces)),
             dma((slab_count - 1,)),
             dma((slab_count - 1,)),
-            dma((total - 1,)),
-            dma((total - 1,)),
+            dma((max(dp_count - 1, 1),)),
+            dma((max(dp_count - 1, 1),)),
         ],
         compiler_params=pltpu.CompilerParams(
             collective_id=0, has_side_effects=True, vmem_limit_bytes=56 * 1024 * 1024
@@ -331,6 +370,15 @@
     )(
         out_weight, rotation, blocks.T, features[0], target[0], wedge, jnp.asarray(hartley_tables(length)),
     )
+    vol_grad, w_grad = pl.pallas_call(
+        hand_over,
+        out_shape=(
+            jax.ShapeDtypeStruct(vol_grad.shape, jnp.float32),
+            jax.ShapeDtypeStruct(w_grad.shape, jnp.float32),
+        ),
+        in_specs=[vmem, vmem],
+        out_specs=(vmem, vmem),
+    )(vol_grad, w_grad)
     return vol_grad[None], w_grad[0]
 
 

time: 37 us -> 35.1 us (0.949)
  local copies, waits for them, and re-layouts: 2.8 us -> 0 us
  Pallas kernels: 32.7 us -> 33.6 us
    unnamed x2 -> x0, local copies, waits for them, and re-layouts: 2.8 us -> none
    pallas_call x0 -> x1, Pallas kernels: none -> 1.68 us  [split_planes(): pl.pallas_call(hand_over, out_shape=(jax.ShapeDtypeStruct(vol_grad.shape,...]
    pallas_call x1, Pallas kernels: 32.7 us -> 31.9 us  [split_planes(): pl.pallas_call(functools.partial(kernel, dp_count, slab_count, float(voxe...]
where the time goes in v1:
time: 35.1 us; the launch traced here: 34.9 us
  Pallas kernels  33.6 us (96%)
  between operations  1.29 us (4%)
    pallas_call x1, Pallas kernels, split_planes(): pl.pallas_call(functools.partial(kernel, dp_count, slab_count, float(voxe...  31.9 us
    pallas_call x1, Pallas kernels, split_planes(): pl.pallas_call(hand_over, out_shape=(jax.ShapeDtypeStruct(vol_grad.shape,...  1.68 us

profile of v1, /device:TPU:0, one launch (start us, length us, event | category | flops | bytes accessed | tf_op | source)
XLA Modules:
  0.0 34.9 jit_solution(16950522649958189414)
XLA Ops:
  1.3 31.9 %shard_map.86 = (f32[32,8,256]{2,1,0:T(8,128)}, f32[1,64]{1,0:T(1,128)}) custom-call(f32[64]{0:T(128)} %weight.1, s32[1]{0:T(128)S(6)} %copy.9.rotation, s32[2,8]{1,0:T(2,128)} %bitcast.7, bf16[64,32,8,256]{3,2,1,0:T(8,128)(2,1)} %bitcast.5, bf16[32,8,256]{2,1,0:T(8,128)(2,1)} %bitcast.6, s32[256,256]{1,0:T(8,128)} %wedge_hbm.1, ...), custom_call_target="tpu_custom_call" | custom-call | tf_op jit(solution)/shard_map/pallas_call | solution.py:333
  33.2 1.7 %shard_map.87 = (f32[32,8,256]{2,1,0:T(8,128)}, f32[1,64]{1,0:T(1,128)}) custom-call(f32[32,8,256]{2,1,0:T(8,128)} %get-tuple-element.6.vol_grad, f32[1,64]{1,0:T(1,128)} %get-tuple-element.7.w_grad), custom_call_target="tpu_custom_call" | custom-call | tf_op jit(solution)/shard_map/pallas_call | solution.py:373

commit v2 on v1

--- a/solution.py
+++ b/solution.py
@@ -126,8 +126,8 @@
     dp_count, slab_count, voxel_count,
     weight, rotation, blocks, features_hbm, target_hbm, wedge_hbm, tables_hbm,
     out_hbm, out_sums,
-    features, target, wedge, tables, out, outgoing, plane, filt, back, returned, sums, own_sum, slab_sums, dp_sums,
-    load_sem, side_sem, send_sem, recv_sem, send2_sem, recv2_sem, sum_send_sem, sum_recv_sem, dp_send_sem, dp_recv_sem,
+    features, target, wedge, tables, out, outgoing, plane, filt, back, returned, sums, own_sum, all_sums,
+    load_sem, side_sem, send_sem, recv_sem, send2_sem, recv2_sem, sum_send_sem, sum_recv_sem,
 ):
     channels, depth, planes, length = features.shape
     pieces = depth // ROWS
@@ -280,39 +280,26 @@
         )
     row_sum = row_sum[0:1]
     own_sum[0] = row_sum
+    place = my_dp * slab_count + me
     sends = []
-    for r in slab_steps:
-        copy = pltpu.make_async_remote_copy(
-            src_ref=own_sum.at[0],
-            dst_ref=slab_sums.at[me],
-            send_sem=sum_send_sem.at[r - 1],
-            recv_sem=sum_recv_sem.at[r - 1],
-            device_id=(my_dp, slab_peer(r)),
-            device_id_type=MESH,
-        )
-        copy.start()
-        sends.append(copy)
-    slab_sums[me] = row_sum
+    for k in range(dp_count - 1, -1, -1):
+        for r in range(slab_count - 1, -1, -1):
+            if k == 0 and r == 0:
+                continue
+            copy = pltpu.make_async_remote_copy(
+                src_ref=own_sum.at[0],
+                dst_ref=all_sums.at[place],
+                send_sem=sum_send_sem.at[k, r],
+                recv_sem=sum_recv_sem.at[k, r],
+                device_id=(dp_peer(k), slab_peer(r)),
+                device_id_type=MESH,
+            )
+            copy.start()
+            sends.append(copy)
+    all_sums[place] = row_sum
     for copy in sends:
         copy.wait()
-    row_sum = jnp.sum(slab_sums[...], axis=0)
-    own_sum[1] = row_sum
-    sends = []
-    for r in range(1, dp_count):
-        copy = pltpu.make_async_remote_copy(
-            src_ref=own_sum.at[1],
-            dst_ref=dp_sums.at[my_dp],
-            send_sem=dp_send_sem.at[r - 1],
-            recv_sem=dp_recv_sem.at[r - 1],
-            device_id=(dp_peer(r), me),
-            device_id_type=MESH,
-        )
-        copy.start()
-        sends.append(copy)
-    dp_sums[my_dp] = row_sum
-    for copy in sends:
-        copy.wait()
-    out_sums[...] = jnp.sum(dp_sums[...], axis=0) / voxel_count
+    out_sums[...] = jnp.sum(all_sums[...], axis=0) / voxel_count
     stored.wait()
 
 
@@ -350,19 +337,16 @@
             pltpu.VMEM((length, length), jnp.float32),
             pltpu.VMEM((planes, depth, length), jnp.float32),
             pltpu.VMEM((channels, 8, 128), jnp.float32),
-            pltpu.VMEM((2, 1, channels), jnp.float32),
-            pltpu.VMEM((slab_count, 1, channels), jnp.float32),
-            pltpu.VMEM((dp_count, 1, channels), jnp.float32),
+            pltpu.VMEM((1, 1, channels), jnp.float32),
+            pltpu.VMEM((dp_count * slab_count, 1, channels), jnp.float32),
             dma((pieces,)),
             dma((4,)),
             dma((slab_count - 1, pieces)),
             dma((slab_count - 1, pieces)),
             dma((slab_count - 1, pieces)),
             dma((slab_count - 1, pieces)),
-            dma((slab_count - 1,)),
-            dma((slab_count - 1,)),
-            dma((max(dp_count - 1, 1),)),
-            dma((max(dp_count - 1, 1),)),
+            dma((dp_count, slab_count)),
+            dma((dp_count, slab_count)),
         ],
         compiler_params=pltpu.CompilerParams(
             collective_id=0, has_side_effects=True, vmem_limit_bytes=56 * 1024 * 1024

time: 35.1 us -> 33.5 us (0.954)
  Pallas kernels: 33.6 us -> 32 us
    pallas_call x1, Pallas kernels: 31.9 us -> 30.3 us  [split_planes(): pl.pallas_call(functools.partial(kernel, dp_count, slab_count, float(voxe...]
where the time goes in v2:
time: 33.5 us; the launch traced here: 33.3 us
  Pallas kernels  32 us (96%)
  between operations  1.29 us (4%)
    pallas_call x1, Pallas kernels, split_planes(): pl.pallas_call(functools.partial(kernel, dp_count, slab_count, float(voxe...  30.3 us
    pallas_call x1, Pallas kernels, split_planes(): pl.pallas_call(hand_over, out_shape=(jax.ShapeDtypeStruct(vol_grad.shape,...  1.68 us

profile of v2, /device:TPU:0, one launch (start us, length us, event | category | flops | bytes accessed | tf_op | source)
XLA Modules:
  0.0 33.3 jit_solution(13954147371651813442)
XLA Ops:
  1.3 30.3 %shard_map.86 = (f32[32,8,256]{2,1,0:T(8,128)}, f32[1,64]{1,0:T(1,128)}) custom-call(f32[64]{0:T(128)} %weight.1, s32[1]{0:T(128)S(6)} %copy.9.rotation, s32[2,8]{1,0:T(2,128)} %bitcast.7, bf16[64,32,8,256]{3,2,1,0:T(8,128)(2,1)} %bitcast.5, bf16[32,8,256]{2,1,0:T(8,128)(2,1)} %bitcast.6, s32[256,256]{1,0:T(8,128)} %wedge_hbm.1, ...), custom_call_target="tpu_custom_call" | custom-call | tf_op jit(solution)/shard_map/pallas_call | solution.py:320
  31.6 1.7 %shard_map.87 = (f32[32,8,256]{2,1,0:T(8,128)}, f32[1,64]{1,0:T(1,128)}) custom-call(f32[32,8,256]{2,1,0:T(8,128)} %get-tuple-element.6.vol_grad, f32[1,64]{1,0:T(1,128)} %get-tuple-element.7.w_grad), custom_call_target="tpu_custom_call" | custom-call | tf_op jit(solution)/shard_map/pallas_call | solution.py:357

commit v3 on v2

--- a/solution.py
+++ b/solution.py
@@ -227,25 +227,35 @@
     first, second = halves(dot3(values, table(2))), halves(dot3(values, table(3)))
     spectrum = dot3(table(0), first) + dot3(table(1), second)
     kept = halves(spectrum * filt[...])
-    first, second = halves(dot3(table(0), kept)), halves(dot3(table(1), kept))
-    back[...] = dot3(first, table(2)) + dot3(second, table(3))
+
+    half = depth // 2
+
+    def table_rows(k, h):
+        return tuple(
+            part.reshape(slab_count, 2, half, length)[:, h].reshape(slab_count * half, length) for part in table(k)
+        )
 
     sends = []
-    for j in range(pieces):
-        sends.append([])
-        for r in slab_steps:
-            peer = slab_peer(r)
-            copy = pltpu.make_async_remote_copy(
-                src_ref=back.at[pl.ds(pl.multiple_of(peer * depth + j * ROWS, ROWS), ROWS)],
-                dst_ref=returned.at[me, pl.ds(j * ROWS, ROWS)],
-                send_sem=send2_sem.at[r - 1, j],
-                recv_sem=recv2_sem.at[r - 1, j],
-                device_id=(my_dp, peer),
-                device_id_type=MESH,
-            )
-            copy.start()
-            sends[j].append(copy)
-    returned[me] = back[pl.ds(pl.multiple_of(me * depth, ROWS), depth), :]
+    for h in range(2):
+        first = halves(dot3(table_rows(0, h), kept))
+        second = halves(dot3(table_rows(1, h), kept))
+        rows = dot3(first, table(2)) + dot3(second, table(3))
+        back[:, pl.ds(h * half, half), :] = rows.reshape(slab_count, half, length)
+        for j in range(h * pieces // 2, (h + 1) * pieces // 2):
+            sends.append([])
+            for r in slab_steps:
+                peer = slab_peer(r)
+                copy = pltpu.make_async_remote_copy(
+                    src_ref=back.at[peer, pl.ds(j * ROWS, ROWS)],
+                    dst_ref=returned.at[me, pl.ds(j * ROWS, ROWS)],
+                    send_sem=send2_sem.at[r - 1, j],
+                    recv_sem=recv2_sem.at[r - 1, j],
+                    device_id=(my_dp, peer),
+                    device_id_type=MESH,
+                )
+                copy.start()
+                sends[j].append(copy)
+    returned[me] = back[me]
 
     for j in range(pieces):
         base = j * ROWS
@@ -334,7 +344,7 @@
             pltpu.VMEM((planes, depth, length), jnp.float32),
             pltpu.VMEM((length, length), jnp.float32),
             pltpu.VMEM((length, length), jnp.float32),
-            pltpu.VMEM((length, length), jnp.float32),
+            pltpu.VMEM((slab_count, depth, length), jnp.float32),
             pltpu.VMEM((planes, depth, length), jnp.float32),
             pltpu.VMEM((channels, 8, 128), jnp.float32),
             pltpu.VMEM((1, 1, channels), jnp.float32),
@@ -373,7 +383,7 @@
             samples == 1
             and planes == 8
             and planes == mesh.shape["slab"]
-            and depth % ROWS == 0
+            and depth % (4 * ROWS) == 0
             and length % 128 == 0
         )
         return (split_planes if whole_planes else split_lines)(features, *rest)

time: 33.5 us -> 33.2 us (level)
  no operation moved by 1% of the time
where the time goes in v3:
time: 33.2 us; the launch traced here: 33.1 us
  Pallas kernels  31.8 us (96%)
  between operations  1.29 us (4%)
    pallas_call x1, Pallas kernels, split_planes(): pl.pallas_call(functools.partial(kernel, dp_count, slab_count, float(voxe...  30.1 us
    pallas_call x1, Pallas kernels, split_planes(): pl.pallas_call(hand_over, out_shape=(jax.ShapeDtypeStruct(vol_grad.shape,...  1.68 us

profile of v3, /device:TPU:0, one launch (start us, length us, event | category | flops | bytes accessed | tf_op | source)
XLA Modules:
  0.0 33.1 jit_solution(2740746102599809508)
XLA Ops:
  1.3 30.1 %shard_map.86 = (f32[32,8,256]{2,1,0:T(8,128)}, f32[1,64]{1,0:T(1,128)}) custom-call(f32[64]{0:T(128)} %weight.1, s32[1]{0:T(128)S(6)} %copy.9.rotation, s32[2,8]{1,0:T(2,128)} %bitcast.7, bf16[64,32,8,256]{3,2,1,0:T(8,128)(2,1)} %bitcast.5, bf16[32,8,256]{2,1,0:T(8,128)(2,1)} %bitcast.6, s32[256,256]{1,0:T(8,128)} %wedge_hbm.1, ...), custom_call_target="tpu_custom_call" | custom-call | tf_op jit(solution)/shard_map/pallas_call | solution.py:330
  31.4 1.7 %shard_map.87 = (f32[32,8,256]{2,1,0:T(8,128)}, f32[1,64]{1,0:T(1,128)}) custom-call(f32[32,8,256]{2,1,0:T(8,128)} %get-tuple-element.6.vol_grad, f32[1,64]{1,0:T(1,128)} %get-tuple-element.7.w_grad), custom_call_target="tpu_custom_call" | custom-call | tf_op jit(solution)/shard_map/pallas_call | solution.py:367

commit v4 on v3

--- a/solution.py
+++ b/solution.py
@@ -217,18 +217,23 @@
     filt[...] = jnp.where(is_odd, odd, even) * (1.0 / (length * length))
     sides[2].wait()
 
-    for copy in sends:
-        copy.wait()
-
     def table(k):
         return tables[2 * k], tables[2 * k + 1]
 
-    values = halves(plane[...])
-    first, second = halves(dot3(values, table(2))), halves(dot3(values, table(3)))
+    half = depth // 2
+    lines = []
+    for h in range(2):
+        for copy in sends[:slab_count - 1] if h == 0 else sends[slab_count - 1:]:
+            copy.wait()
+        values = halves(jnp.concatenate(
+            [plane[q * depth + h * half:q * depth + (h + 1) * half, :] for q in range(slab_count)], axis=0
+        ))
+        lines.append([dot3(values, table(k)).reshape(slab_count, half, length) for k in (2, 3)])
+    first, second = (
+        halves(jnp.stack([lines[0][k], lines[1][k]], axis=1).reshape(length, length)) for k in range(2)
+    )
     spectrum = dot3(table(0), first) + dot3(table(1), second)
     kept = halves(spectrum * filt[...])
-
-    half = depth // 2
 
     def table_rows(k, h):
         return tuple(
@@ -383,7 +388,7 @@
             samples == 1
             and planes == 8
             and planes == mesh.shape["slab"]
-            and depth % (4 * ROWS) == 0
+            and depth == 2 * HELD * ROWS
             and length % 128 == 0
         )
         return (split_planes if whole_planes else split_lines)(features, *rest)

time: 33.2 us -> 33.1 us (level)
  no operation moved by 1% of the time
where the time goes in v4:
time: 33.1 us; the launch traced here: 33 us
  Pallas kernels  31.7 us (96%)
  between operations  1.29 us (4%)
    pallas_call x1, Pallas kernels, split_planes(): pl.pallas_call(functools.partial(kernel, dp_count, slab_count, float(voxe...  30 us
    pallas_call x1, Pallas kernels, split_planes(): pl.pallas_call(hand_over, out_shape=(jax.ShapeDtypeStruct(vol_grad.shape,...  1.68 us

profile of v4, /device:TPU:0, one launch (start us, length us, event | category | flops | bytes accessed | tf_op | source)
XLA Modules:
  0.0 33.0 jit_solution(5745873325223104469)
XLA Ops:
  1.3 30.0 %shard_map.86 = (f32[32,8,256]{2,1,0:T(8,128)}, f32[1,64]{1,0:T(1,128)}) custom-call(f32[64]{0:T(128)} %weight.1, s32[1]{0:T(128)S(6)} %copy.9.rotation, s32[2,8]{1,0:T(2,128)} %bitcast.7, bf16[64,32,8,256]{3,2,1,0:T(8,128)(2,1)} %bitcast.5, bf16[32,8,256]{2,1,0:T(8,128)(2,1)} %bitcast.6, s32[256,256]{1,0:T(8,128)} %wedge_hbm.1, ...), custom_call_target="tpu_custom_call" | custom-call | tf_op jit(solution)/shard_map/pallas_call | solution.py:335
  31.3 1.7 %shard_map.87 = (f32[32,8,256]{2,1,0:T(8,128)}, f32[1,64]{1,0:T(1,128)}) custom-call(f32[32,8,256]{2,1,0:T(8,128)} %get-tuple-element.6.vol_grad, f32[1,64]{1,0:T(1,128)} %get-tuple-element.7.w_grad), custom_call_target="tpu_custom_call" | custom-call | tf_op jit(solution)/shard_map/pallas_call | solution.py:372
